TPU v7x, 32 devices: a whole 2x2x4 slice. The times are simulated.
32 devices in a mesh: dp: 8 (over z, y), tensor: 4 (over x, core).
Axes of the slice: x: 2, y: 2, z: 4, core: 2. Of those that a mesh axis runs over, the one named last changes fastest.
Arguments:
- tokens: bfloat16 [16384, 1024], P(('dp', 'tensor')), may hold values from -6 to 6
- output_cotangent: bfloat16 [16384, 1024], P(('dp', 'tensor')), may hold values from -6 to 6
- lengths: int32 [8], P('dp'), may hold values from 1024 to 2048, as said below
- block_place: int32 [8, 32], P('dp'), may hold values from 0 to 31, each once within a row
- random_blocks: int32 [8, 16, 32, 3], P('dp', 'tensor'), may hold values from 0 to 31
- qkv_weight: bfloat16 [1024, 3, 1024], P('dp', None, 'tensor'), may hold values from -0.1875 to 0.1875
- out_weight: bfloat16 [1024, 1024], P('dp', 'tensor'), may hold values from -0.75 to 0.75
- up_weight: bfloat16 [1024, 4096], P('dp', 'tensor'), may hold values from -0.1875 to 0.1875
- down_weight: bfloat16 [1024, 4096], P('dp', 'tensor'), may hold values from -0.09375 to 0.09375
- vectors: float32 [8, 1024], P(None, ('dp', 'tensor')), may hold values from -2 to 2
- hidden_bias: float32 [1, 4096], P(None, ('dp', 'tensor')), may hold values from -3 to 3
Outputs:
- output: bfloat16 [16384, 1024], P(('dp', 'tensor'))
- input_grad: bfloat16 [16384, 1024], P(('dp', 'tensor'))
- qkv_weight_grad: float32 [1024, 3, 1024], P('dp', None, 'tensor')
- out_weight_grad: float32 [1024, 1024], P('dp', 'tensor')
- up_weight_grad: float32 [1024, 4096], P('dp', 'tensor')
- down_weight_grad: float32 [1024, 4096], P('dp', 'tensor')
- vectors_grad: float32 [8, 1024], P(None, ('dp', 'tensor'))
- hidden_bias_grad: float32 [1, 4096], P(None, ('dp', 'tensor'))
Inputs may be any that keep to these rules, and one draw needn't show every extreme that they name: `lengths`: one sequence has exactly 2048 tokens. `block_place`: each row is a permutation.
All inputs are finite; a program needn't handle non-finite values.
Results may differ from a plain program's by a relative error of at most 0.015.
Values may be sent and summed in bfloat16 or wider, within the bound.
No kernel may reach another device: no remote copies, remote signals or barrier semaphores. Data moves between devices by JAX's collectives and lax.ppermute only.
A program may use at most 192 MiB of HBM per device.

v0:
```python
import math
import jax
import jax.numpy as jnp
from jax import lax
from jax.sharding import PartitionSpec as P

HEAD_DIM = 64
BLOCK = 64
EPS = 1e-05
NEGATIVE = -1e30


def in_blocks(value, dim, count):
    before, after = (value.shape[:dim], value.shape[dim + 1 :])
    return jnp.moveaxis(value.reshape(*before, count, -1, *after), dim, 0)


def sent_and_summed(value, axis, dim):
    count = lax.axis_size(axis)
    blocks = lax.all_to_all(in_blocks(value, dim, count), axis, 0, 0, tiled=True)
    return jnp.sum(blocks.astype(jnp.float32), axis=0)


def in_one_piece(arrays, axis, dim, along):
    widths = [math.prod(a.shape[along:]) for a in arrays]
    both = jnp.concatenate(
        [a.reshape(*a.shape[:along], w) for a, w in zip(arrays, widths)], axis=along
    )
    result = sent_and_summed(both, axis, dim)
    blocks = jnp.split(result, [sum(widths[:k]) for k in range(1, len(widths))], axis=along)
    return tuple(
        (b.reshape(*result.shape[:along], *a.shape[along:]) for a, b in zip(arrays, blocks))
    )


def layer_norm_parts(input_rows, gain_row, shift_row):
    centred = input_rows - jnp.mean(input_rows, axis=-1, keepdims=True)
    inverse = lax.rsqrt(jnp.mean(centred * centred, axis=-1, keepdims=True) + EPS)
    unit_rows = centred * inverse
    return (unit_rows * gain_row + shift_row, unit_rows, inverse)


def layer_norm_back(grad_normed, unit_rows, inverse, gain_row):
    grad_unit = grad_normed * gain_row
    grad_rows = inverse * (
        grad_unit
        - jnp.mean(grad_unit, axis=-1, keepdims=True)
        - unit_rows * jnp.mean(grad_unit * unit_rows, axis=-1, keepdims=True)
    )
    return (grad_rows, jnp.sum(grad_normed * unit_rows, axis=0), jnp.sum(grad_normed, axis=0))


def gelu_tanh(pre_active):
    return jax.nn.gelu(pre_active, approximate=True)


def gather_rows(local_rows):
    return lax.all_gather(local_rows, "tensor", axis=0, tiled=True)


def sum_rows(partial_rows):
    return lax.psum_scatter(
        partial_rows.astype(jnp.bfloat16), "tensor", scatter_dimension=0, tiled=True
    ).astype(jnp.float32)


def attention_weights(qkv_weight, out_weight):
    return (
        lax.all_gather(qkv_weight, "dp", axis=0, tiled=True),
        lax.all_gather(out_weight, "dp", axis=0, tiled=True),
    )


def feed_weights(up_weight, down_weight):
    return (
        lax.all_gather(up_weight, "dp", axis=0, tiled=True),
        lax.all_gather(down_weight, "dp", axis=0, tiled=True),
    )


def block_masks(length, placing, chosen):
    nblocks = (length + BLOCK - 1) // BLOCK
    query_seq = placing[:, None]
    key_seq = placing[None, :]
    common = (
        (query_seq == 0)
        | (query_seq == nblocks - 1)
        | (key_seq == 0)
        | (key_seq == nblocks - 1)
        | (jnp.abs(query_seq - key_seq) <= 1)
    )
    by_query = jnp.take(chosen, placing, axis=1)
    random_hit = jnp.any(by_query[:, :, None, :] == key_seq[None, :, :, None], axis=-1)
    allowed = common[None] | random_hit
    positions = placing[:, None] * BLOCK + jnp.arange(BLOCK, dtype=jnp.int32)[None, :]
    return (allowed, positions < length)


def tile_scores(query_tile, key_rows, allowed_tile, key_valid, score_scale):
    scores = (
        jnp.einsum("qhd,khd->hqk", query_tile, key_rows, preferred_element_type=jnp.float32)
        * score_scale
    )
    heads_here = allowed_tile.shape[0]
    blocks_here = allowed_tile.shape[1]
    block_size = key_valid.shape[1]
    scores = scores.reshape(heads_here, blocks_here, block_size, key_valid.shape[0], block_size)
    keep_mask = allowed_tile[:, :, None, :, None] & key_valid[None, None, None, :, :]
    scores = jnp.where(keep_mask, scores, NEGATIVE)
    return scores.reshape(heads_here, blocks_here * block_size, -1)


def project_heads(normed_all, qkv_full, bias_query, bias_value):
    projected = jnp.einsum("td,dcf->ctf", normed_all, qkv_full, preferred_element_type=jnp.float32)
    head_shape = (normed_all.shape[0], -1, HEAD_DIM)
    queries = (projected[0] + bias_query).astype(jnp.bfloat16).reshape(head_shape)
    key_rows = projected[1].astype(jnp.bfloat16).reshape(head_shape)
    value_rows = (projected[2] + bias_value).astype(jnp.bfloat16).reshape(head_shape)
    return (queries, key_rows, value_rows)


def attend(queries, key_rows, value_rows, allowed, key_valid, tile_rows, score_scale):
    per_tile = tile_rows // BLOCK

    def one_tile(number):
        query_tile = lax.dynamic_slice_in_dim(queries, number * tile_rows, tile_rows, 0)
        allowed_tile = lax.dynamic_slice_in_dim(allowed, number * per_tile, per_tile, 1)
        scores = tile_scores(query_tile, key_rows, allowed_tile, key_valid, score_scale)
        row_top = jnp.max(scores, axis=-1, keepdims=True)
        weights = jnp.exp(scores - row_top)
        row_total = jnp.sum(weights, axis=-1, keepdims=True)
        probabilities = (weights / row_total).astype(jnp.bfloat16)
        context_tile = jnp.einsum(
            "hqk,khd->qhd", probabilities, value_rows, preferred_element_type=jnp.float32
        )
        return (
            context_tile.reshape(tile_rows, -1).astype(jnp.bfloat16),
            (row_top + jnp.log(row_total))[..., 0],
        )

    context_tiles, log_totals = lax.map(
        one_tile, jnp.arange(queries.shape[0] // tile_rows, dtype=jnp.int32)
    )
    return (context_tiles.reshape(queries.shape[0], -1), log_totals)


def attend_back(
    queries,
    key_rows,
    value_rows,
    grad_context,
    log_totals,
    allowed,
    key_valid,
    tile_rows,
    score_scale,
):
    per_tile = tile_rows // BLOCK

    def one_tile(state_pair, number):
        grad_keys, grad_values = state_pair
        query_tile = lax.dynamic_slice_in_dim(queries, number * tile_rows, tile_rows, 0)
        grad_tile = lax.dynamic_slice_in_dim(grad_context, number * tile_rows, tile_rows, 0)
        allowed_tile = lax.dynamic_slice_in_dim(allowed, number * per_tile, per_tile, 1)
        scores = tile_scores(query_tile, key_rows, allowed_tile, key_valid, score_scale)
        probabilities = jnp.exp(scores - log_totals[number][:, :, None])
        probs_low = probabilities.astype(jnp.bfloat16)
        grad_probs = jnp.einsum(
            "qhd,khd->hqk", grad_tile, value_rows, preferred_element_type=jnp.float32
        )
        row_inner = jnp.sum(probabilities * grad_probs, axis=-1, keepdims=True)
        grad_scores = (probabilities * (grad_probs - row_inner)).astype(jnp.bfloat16)
        grad_query = (
            jnp.einsum("hqk,khd->qhd", grad_scores, key_rows, preferred_element_type=jnp.float32)
            * score_scale
        )
        grad_keys = (
            grad_keys
            + jnp.einsum(
                "hqk,qhd->khd", grad_scores, query_tile, preferred_element_type=jnp.float32
            )
            * score_scale
        )
        grad_values = grad_values + jnp.einsum(
            "hqk,qhd->khd", probs_low, grad_tile, preferred_element_type=jnp.float32
        )
        return ((grad_keys, grad_values), grad_query.astype(jnp.bfloat16))

    zero_state = jnp.zeros(key_rows.shape, jnp.float32)
    final_state, grad_queries = lax.scan(
        one_tile,
        (zero_state, zero_state),
        jnp.arange(queries.shape[0] // tile_rows, dtype=jnp.int32),
    )
    flat_queries = grad_queries.reshape(queries.shape[0], -1)
    flat_keys = final_state[0].reshape(flat_queries.shape).astype(jnp.bfloat16)
    flat_values = final_state[1].reshape(flat_queries.shape).astype(jnp.bfloat16)
    return (flat_queries, flat_keys, flat_values)


def per_device(
    tokens,
    output_cotangent,
    lengths,
    block_place,
    random_blocks,
    qkv_weight,
    out_weight,
    up_weight,
    down_weight,
    vectors,
    hidden_bias,
):
    vectors_full, hidden_full = (
        lax.all_gather(vectors, ("dp", "tensor"), axis=1, tiled=True),
        lax.all_gather(hidden_bias, ("dp", "tensor"), axis=1, tiled=True),
    )
    width_local = qkv_weight.shape[2]
    units_local = up_weight.shape[1]
    position = lax.axis_index("tensor")
    head_start = position * width_local
    unit_start = position * units_local
    bias_query = lax.dynamic_slice_in_dim(vectors_full[6], head_start, width_local)
    bias_value = lax.dynamic_slice_in_dim(vectors_full[7], head_start, width_local)
    bias_hidden = lax.dynamic_slice_in_dim(hidden_full[0], unit_start, units_local)
    allowed, key_valid = block_masks(lengths[0], block_place[0], random_blocks[0])
    slot_rows = tokens.shape[0] * lax.axis_size("tensor")
    tile_rows = min(512, slot_rows)
    score_scale = HEAD_DIM ** (-0.5)
    residual_in = tokens.astype(jnp.float32)
    qkv_full, out_full = attention_weights(qkv_weight, out_weight)
    normed_one, unit_one, inverse_one = layer_norm_parts(
        residual_in, vectors_full[0], vectors_full[1]
    )
    normed_one_all = gather_rows(normed_one.astype(jnp.bfloat16))
    queries, key_rows, value_rows = project_heads(normed_one_all, qkv_full, bias_query, bias_value)
    context, log_totals = attend(
        queries, key_rows, value_rows, allowed, key_valid, tile_rows, score_scale
    )
    attended = sum_rows(
        jnp.einsum("tf,df->td", context, out_full, preferred_element_type=jnp.float32)
    )
    middle = residual_in + attended + vectors_full[4]
    normed_two, unit_two, inverse_two = layer_norm_parts(middle, vectors_full[2], vectors_full[3])
    up_full, down_full = feed_weights(up_weight, down_weight)
    normed_two_all = gather_rows(normed_two.astype(jnp.bfloat16))
    hidden = jnp.dot(normed_two_all, up_full, preferred_element_type=jnp.float32) + bias_hidden
    active = gelu_tanh(hidden).astype(jnp.bfloat16)
    feed_out = sum_rows(
        jnp.einsum("tf,df->td", active, down_full, preferred_element_type=jnp.float32)
    )
    output = (middle + feed_out + vectors_full[5]).astype(jnp.bfloat16)
    grad_all = gather_rows(output_cotangent)
    up_back, down_back = feed_weights(up_weight, down_weight)
    normed_two_back = gather_rows(normed_two.astype(jnp.bfloat16))
    hidden_back = (
        jnp.dot(normed_two_back, up_back, preferred_element_type=jnp.float32) + bias_hidden
    )
    active_back = gelu_tanh(hidden_back).astype(jnp.bfloat16)
    grad_active = jnp.dot(grad_all, down_back, preferred_element_type=jnp.float32)
    gelu_pullback = jax.vjp(gelu_tanh, hidden_back)[1]
    grad_hidden = gelu_pullback(grad_active)[0].astype(jnp.bfloat16)
    grad_up = jnp.einsum(
        "td,tf->df", normed_two_back, grad_hidden, preferred_element_type=jnp.float32
    )
    grad_down = jnp.einsum("td,tf->df", grad_all, active_back, preferred_element_type=jnp.float32)
    grad_bias_hidden = jnp.sum(grad_hidden, axis=0, dtype=jnp.float32)
    grad_normed_two = sum_rows(
        jnp.einsum("tf,df->td", grad_hidden, up_back, preferred_element_type=jnp.float32)
    )
    up_weight_grad, down_weight_grad = (
        lax.psum_scatter(grad_up, "dp", scatter_dimension=0, tiled=True),
        lax.psum_scatter(grad_down, "dp", scatter_dimension=0, tiled=True),
    )
    cotangent_rows = output_cotangent.astype(jnp.float32)
    grad_middle_part, grad_gain_two, grad_shift_two = layer_norm_back(
        grad_normed_two, unit_two, inverse_two, vectors_full[2]
    )
    grad_middle = cotangent_rows + grad_middle_part
    grad_attended_all = gather_rows(grad_middle.astype(jnp.bfloat16))
    qkv_back, out_back = attention_weights(qkv_weight, out_weight)
    normed_one_back = gather_rows(normed_one.astype(jnp.bfloat16))
    queries_back, keys_back, values_back = project_heads(
        normed_one_back, qkv_back, bias_query, bias_value
    )
    grad_context = jnp.dot(grad_attended_all, out_back, preferred_element_type=jnp.float32).astype(
        jnp.bfloat16
    )
    grad_out_weight = jnp.einsum(
        "td,tf->df", grad_attended_all, context, preferred_element_type=jnp.float32
    )
    grad_context_heads = grad_context.reshape(slot_rows, -1, HEAD_DIM)
    grad_queries, grad_keys, grad_values = attend_back(
        queries_back,
        keys_back,
        values_back,
        grad_context_heads,
        log_totals,
        allowed,
        key_valid,
        tile_rows,
        score_scale,
    )
    grad_projected = jnp.stack([grad_queries, grad_keys, grad_values])
    grad_qkv = jnp.einsum(
        "td,ctf->dcf", normed_one_back, grad_projected, preferred_element_type=jnp.float32
    )
    grad_normed_one = sum_rows(
        jnp.einsum("ctf,dcf->td", grad_projected, qkv_back, preferred_element_type=jnp.float32)
    )
    qkv_weight_grad, out_weight_grad = in_one_piece(
        (grad_qkv.astype(jnp.bfloat16), grad_out_weight.astype(jnp.bfloat16)), "dp", 0, 1
    )
    grad_input_part, grad_gain_one, grad_shift_one = layer_norm_back(
        grad_normed_one, unit_one, inverse_one, vectors_full[0]
    )
    input_grad = (grad_middle + grad_input_part).astype(jnp.bfloat16)
    local_grads = jnp.stack(
        [
            grad_gain_one,
            grad_shift_one,
            grad_gain_two,
            grad_shift_two,
            jnp.sum(grad_middle, axis=0),
            jnp.sum(cotangent_rows, axis=0),
        ]
    )
    head_bias_grads = jnp.stack(
        [
            jnp.sum(grad_queries, axis=0, dtype=jnp.float32),
            jnp.sum(grad_values, axis=0, dtype=jnp.float32),
        ]
    )
    head_grads = lax.dynamic_update_slice(
        jnp.zeros((2, vectors_full.shape[1]), jnp.float32), head_bias_grads, (0, head_start)
    )
    hidden_grads = lax.dynamic_update_slice(
        jnp.zeros(hidden_full.shape, jnp.float32), grad_bias_hidden[None, :], (0, unit_start)
    )
    vectors_grad, hidden_bias_grad = (
        lax.psum_scatter(
            jnp.concatenate([local_grads, head_grads], axis=0),
            ("dp", "tensor"),
            scatter_dimension=1,
            tiled=True,
        ),
        lax.psum_scatter(hidden_grads, ("dp", "tensor"), scatter_dimension=1, tiled=True),
    )
    return (
        output,
        input_grad,
        qkv_weight_grad,
        out_weight_grad,
        up_weight_grad,
        down_weight_grad,
        vectors_grad,
        hidden_bias_grad,
    )


def solution(mesh):
    placed = (
        P(("dp", "tensor"), None),
        P(("dp", "tensor"), None),
        P("dp"),
        P("dp", None),
        P("dp", "tensor", None, None),
        P("dp", None, "tensor"),
        P("dp", "tensor"),
        P("dp", "tensor"),
        P("dp", "tensor"),
        P(None, ("dp", "tensor")),
        P(None, ("dp", "tensor")),
    )
    return jax.shard_map(
        per_device,
        mesh=mesh,
        in_specs=placed,
        out_specs=(
            P(("dp", "tensor"), None),
            P(("dp", "tensor"), None),
            P("dp", None, "tensor"),
            P("dp", "tensor"),
            P("dp", "tensor"),
            P("dp", "tensor"),
            P(None, ("dp", "tensor")),
            P(None, ("dp", "tensor")),
        ),
        check_vma=False,
    )
```

profile of v0, /device:TPU:0, one launch (start us, length us, event | category | flops | bytes accessed | tf_op | source)
XLA Modules:
  0.0 1534.6 jit_solution(7175553528561986382)
XLA Ops:
  9.1 44.2 %all-gather = f32[32,32,8]{1,2,0:T(8,128)S(1)} all-gather(f32[1,32,8]{1,2,0:T(8,128)} %bitcast.196), channel_id=1, replica_groups=mesh['dp'=8,'tensor'=4] {'dp','tensor'}, dimensions={0}, use_global_device_ids=true | all-gather | bytes 33792 | tf_op jit(solution)/shard_map/all_gather | solution.py:215
  62.7 33.9 %all_gather.39 = bf16[1024,256]{1,0:T(8,128)(2,1)} all-gather(bf16[128,256]{1,0:T(8,128)(2,1)S(1)} %copy-done.18), channel_id=1, replica_groups=mesh['dp'=8,'tensor'=4] {'dp'}, dimensions={0}, use_global_device_ids=true | all-gather | bytes 589824 | tf_op jit(solution)/shard_map/all_gather | solution.py:70
  104.3 192.3 %while.28 = (s32[]{:T(128)}, bf16[4,512,256]{2,1,0:T(8,128)(2,1)}, f32[4,4,512]{2,1,0:T(4,128)S(1)}, s32[4]{0:T(128)S(1)}, pred[4,32,32]{2,1,0:T(8,128)(4,1)S(1)...) while((s32[]{:T(128)}, bf16[4,512,256]{2,1,0:T(8,128)(2,1)}, ...), condition=%wide.region_6.7_spmd.clone, body=%wide.region_3.6_spmd.clone.sunk | while | flops 1124272128 | bytes 96148904 | solution.py:141
  112.5 22.8 %broadcast_in_dim.121 = pred[4,512,2048]{2,1,0:T(32,128)(4,1)} reshape(pred[4,8,64,32,64]{4,3,2,1,0:T(32,128)(4,1)} %broadcast_in_dim.120) | data formatting | bytes 8388608 | tf_op jit(solution)/shard_map/while/body/eval_jaxpr/jit(_where)/broadcast_in_dim | solution.py:109
  160.5 22.8 %broadcast_in_dim.121 = pred[4,512,2048]{2,1,0:T(32,128)(4,1)} reshape(pred[4,8,64,32,64]{4,3,2,1,0:T(32,128)(4,1)} %broadcast_in_dim.120) | data formatting | bytes 8388608 | tf_op jit(solution)/shard_map/while/body/eval_jaxpr/jit(_where)/broadcast_in_dim | solution.py:109
  208.6 22.8 %broadcast_in_dim.121 = pred[4,512,2048]{2,1,0:T(32,128)(4,1)} reshape(pred[4,8,64,32,64]{4,3,2,1,0:T(32,128)(4,1)} %broadcast_in_dim.120) | data formatting | bytes 8388608 | tf_op jit(solution)/shard_map/while/body/eval_jaxpr/jit(_where)/broadcast_in_dim | solution.py:109
  256.7 22.8 %broadcast_in_dim.121 = pred[4,512,2048]{2,1,0:T(32,128)(4,1)} reshape(pred[4,8,64,32,64]{4,3,2,1,0:T(32,128)(4,1)} %broadcast_in_dim.120) | data formatting | bytes 8388608 | tf_op jit(solution)/shard_map/while/body/eval_jaxpr/jit(_where)/broadcast_in_dim | solution.py:109
  301.9 41.5 %reduce-scatter.13.cloned.1.call-done = bf16[512,1024]{1,0:T(8,128)(2,1)} async-done(((bf16[2048,1024]{1,0:T(8,128)(2,1)}), bf16[512,1024]{1,0:T(8,128)(2,1)}) %reduce-scatter.13.cloned.1.call-update) | async-done | bytes 1048592 | tf_op jit(solution)/shard_map/reduce_scatter | solution.py:62
  349.9 40.5 %all_gather.42 = f32[1,4096]{1,0:T(1,128)S(1)} all-gather(f32[1,128]{1,0:T(1,128)S(1)} %copy-done.36), channel_id=1, replica_groups=mesh['dp'=8,'tensor'=4] {'dp','tensor'}, dimensions={1}, use_global_device_ids=true | all-gather | bytes 16896 | tf_op jit(solution)/shard_map/all_gather | solution.py:216
  394.9 35.1 %all-gather.13.cloned.1.call-done = bf16[2048,1024]{1,0:T(8,128)(2,1)} async-done(((bf16[512,1024]{1,0:T(8,128)(2,1)}), bf16[2048,1024]{1,0:T(8,128)(2,1)}) %all-gather.13.cloned.1.call-update) | async-done | bytes 4194320 | tf_op jit(solution)/shard_map/all_gather | solution.py:58
  440.6 40.9 %all-gather.17.cloned.1.call-done = bf16[1024,1024]{1,0:T(8,128)(2,1)} async-done(((bf16[128,1024]{1,0:T(8,128)(2,1)}), bf16[1024,1024]{1,0:T(8,128)(2,1)}) %all-gather.17.cloned.1.call-update) | async-done | bytes 2097168 | tf_op jit(solution)/shard_map/all_gather | solution.py:77
  481.5 34.6 %all-gather.19.cloned.1.call-done = bf16[2048,1024]{1,0:T(8,128)(2,1)} async-done(((bf16[512,1024]{1,0:T(8,128)(2,1)}), bf16[2048,1024]{1,0:T(8,128)(2,1)}) %all-gather.19.cloned.1.call-update) | async-done | bytes 4194320 | tf_op jit(solution)/shard_map/all_gather | solution.py:58
  516.1 14.3 convert_reduce_fusion
  539.1 11.7 convolution_convert_fusion.2
  550.9 32.6 %reduce-scatter.17.cloned.1.call-done = bf16[512,1024]{1,0:T(8,128)(2,1)} async-done(((bf16[2048,1024]{1,0:T(8,128)(2,1)}), bf16[512,1024]{1,0:T(8,128)(2,1)}) %reduce-scatter.17.cloned.1.call-update) | async-done | bytes 1048592 | tf_op jit(solution)/shard_map/reduce_scatter | solution.py:62
  586.8 43.7 %reduce-scatter.15.cloned.1.call-done = bf16[512,1024]{1,0:T(8,128)(2,1)} async-done(((bf16[2048,1024]{1,0:T(8,128)(2,1)}), bf16[512,1024]{1,0:T(8,128)(2,1)}) %reduce-scatter.15.cloned.1.call-update) | async-done | bytes 1048592 | tf_op jit(solution)/shard_map/reduce_scatter | solution.py:62
  637.6 34.6 %all-gather.21.cloned.1.call-done = bf16[2048,1024]{1,0:T(8,128)(2,1)} async-done(((bf16[512,1024]{1,0:T(8,128)(2,1)}), bf16[2048,1024]{1,0:T(8,128)(2,1)}) %all-gather.21.cloned.1.call-update) | async-done | bytes 4194320 | tf_op jit(solution)/shard_map/all_gather | solution.py:58
  676.7 328.6 %while.29 = (s32[]{:T(128)}, f32[2048,4,64]{0,2,1:T(8,128)}, f32[2048,4,64]{0,2,1:T(8,128)}, bf16[4,512,4,64]{1,3,2,0:T(8,128)(2,1)}, s32[4]{0:T(128)S(1)}, /*in...) while((s32[]{:T(128)}, f32[2048,4,64]{0,2,1:T(8,128)}, ...), condition=%wide.region_16.17_spmd.clone, body=%wide.region_14.16_spmd.clone.sunk | while | flops 2725054464 | bytes 256294480 | solution.py:190
  687.1 22.8 %broadcast_in_dim.123 = pred[4,512,2048]{2,1,0:T(32,128)(4,1)} reshape(pred[4,8,64,32,64]{4,3,2,1,0:T(32,128)(4,1)} %broadcast_in_dim.122) | data formatting | bytes 8388608 | tf_op jit(solution)/shard_map/while/body/eval_jaxpr/jit(_where)/broadcast_in_dim | solution.py:109
  719.1 12.7 multiply_reduce_fusion.3
  768.5 22.8 %broadcast_in_dim.123 = pred[4,512,2048]{2,1,0:T(32,128)(4,1)} reshape(pred[4,8,64,32,64]{4,3,2,1,0:T(32,128)(4,1)} %broadcast_in_dim.122) | data formatting | bytes 8388608 | tf_op jit(solution)/shard_map/while/body/eval_jaxpr/jit(_where)/broadcast_in_dim | solution.py:109
  800.6 12.7 multiply_reduce_fusion.3
  850.8 22.8 %broadcast_in_dim.123 = pred[4,512,2048]{2,1,0:T(32,128)(4,1)} reshape(pred[4,8,64,32,64]{4,3,2,1,0:T(32,128)(4,1)} %broadcast_in_dim.122) | data formatting | bytes 8388608 | tf_op jit(solution)/shard_map/while/body/eval_jaxpr/jit(_where)/broadcast_in_dim | solution.py:109
  882.8 12.7 multiply_reduce_fusion.3
  933.0 22.8 %broadcast_in_dim.123 = pred[4,512,2048]{2,1,0:T(32,128)(4,1)} reshape(pred[4,8,64,32,64]{4,3,2,1,0:T(32,128)(4,1)} %broadcast_in_dim.122) | data formatting | bytes 8388608 | tf_op jit(solution)/shard_map/while/body/eval_jaxpr/jit(_where)/broadcast_in_dim | solution.py:109
  965.0 12.7 multiply_reduce_fusion.3
  1030.6 13.3 convolution_bitcast_fusion
  1044.7 27.9 %reduce-scatter.19.cloned.1.call-done = bf16[512,1024]{1,0:T(8,128)(2,1)} async-done(((bf16[2048,1024]{1,0:T(8,128)(2,1)}), bf16[512,1024]{1,0:T(8,128)(2,1)}) %reduce-scatter.19.cloned.1.call-update) | async-done | bytes 1048592 | tf_op jit(solution)/shard_map/reduce_scatter | solution.py:62
  1109.1 105.7 %reduce-scatter.27.cloned.1.call-done = f32[128,1]{1,0:T(8,128)} async-done(((f32[4096,1]{1,0:T(8,128)}), f32[128,1]{1,0:T(8,128)}) %reduce-scatter.27.cloned.1.call-update) | async-done | bytes 528
  1216.2 87.6 %reduce-scatter.23.cloned.1.call-done = f32[128,1024]{0,1:T(8,128)} async-done(((f32[1024,1024]{0,1:T(8,128)}), f32[128,1024]{0,1:T(8,128)}) %reduce-scatter.23.cloned.1.call-update) | async-done | bytes 524304 | tf_op jit(solution)/shard_map/reduce_scatter | solution.py:273
  1314.7 124.8 %reduce-scatter.25.cloned.1.call-done = f32[32,8]{1,0:T(8,128)} async-done(((f32[1024,8]{1,0:T(8,128)}), f32[32,8]{1,0:T(8,128)}) %reduce-scatter.25.cloned.1.call-update) | async-done | bytes 1040
  1440.9 86.9 %reduce-scatter.21.cloned.1.call-done = f32[128,1024]{1,0:T(8,128)} async-done(((f32[1024,1024]{1,0:T(8,128)}), f32[128,1024]{1,0:T(8,128)}) %reduce-scatter.21.cloned.1.call-update) | async-done | bytes 524304 | tf_op jit(solution)/shard_map/reduce_scatter | solution.py:272
  (319 shorter events, 413.4 us)
Async XLA Ops:
  7.2 54.0 %copy-start.32 = (s32[1,4,32,3]{2,1,3,0:T(4,128)S(1)}, s32[1,4,32,3]{2,1,3,0:T(4,128)}, u32[]{:S(2)}) copy-start(s32[1,4,32,3]{2,1,3,0:T(4,128)} %param.19) | copy-start | bytes 4612
  7.2 54.2 %copy-start.31 = (s32[1,32]{1,0:T(1,128)S(1)}, s32[1,32]{1,0:T(1,128)}, u32[]{:S(2)}) copy-start(s32[1,32]{1,0:T(1,128)} %param.18) | copy-start | bytes 388
  7.2 55.5 %copy-start.18 = (bf16[128,256]{1,0:T(8,128)(2,1)S(1)}, bf16[128,256]{1,0:T(8,128)(2,1)}, u32[]{:S(2)}) copy-start(bf16[128,256]{1,0:T(8,128)(2,1)} %param.21) | copy-start | bytes 196612
  7.2 89.3 %all-gather.11.cloned.1.call-start = ((), (), s32[]{:S(2)}) async-start(), calls=%async_computation.10 | async-start | bytes 1769472 | tf_op jit(solution)/shard_map/all_gather | solution.py:69
  9.0 87.5 %all-gather.9.cloned.1.call-start = ((), (), s32[]{:S(2)}) async-start(), calls=%async_computation.9 | async-start | bytes 5242880 | tf_op jit(solution)/shard_map/all_gather | solution.py:58
  60.4 282.9 %reduce-scatter.13.cloned.1.call-start = ((), (), s32[]{:S(2)}) async-start(), calls=%async_computation.11 | async-start | bytes 5242880 | tf_op jit(solution)/shard_map/reduce_scatter | solution.py:62
  104.3 192.3 %copy-start.13 = (bf16[1024,256]{1,0:T(8,128)(2,1)S(1)}, bf16[1024,256]{1,0:T(8,128)(2,1)}, u32[]{:S(2)}) copy-start(bf16[1024,256]{1,0:T(8,128)(2,1)} %all_gather.39) | copy-start | bytes 1572868
  301.0 42.3 %copy-start.3 = (bf16[512,1024]{1,0:T(8,128)(2,1)S(1)}, bf16[512,1024]{1,0:T(8,128)(2,1)}, u32[]{:S(2)}) copy-start(bf16[512,1024]{1,0:T(8,128)(2,1)} %param.15) | copy-start | bytes 3145732
  301.0 42.3 %copy-start.16 = (f32[1,1024]{1,0:T(1,128)S(1)}, f32[1,1024]{1,0:T(1,128)}, u32[]{:S(2)}) copy-start(f32[1,1024]{1,0:T(1,128)} %get-tuple-element.298) | copy-start | bytes 12292
  301.0 45.9 %copy-start.17 = (f32[1,1024]{1,0:T(1,128)S(1)}, f32[1,1024]{1,0:T(1,128)}, u32[]{:S(2)}) copy-start(f32[1,1024]{1,0:T(1,128)} %get-tuple-element.297) | copy-start | bytes 12292
  301.1 45.9 %copy-start.26 = (f32[1,1024]{1,0:T(1,128)S(1)}, f32[1,1024]{1,0:T(1,128)}, u32[]{:S(2)}) copy-start(f32[1,1024]{1,0:T(1,128)} %get-tuple-element.296) | copy-start | bytes 12292
  301.1 93.8 %all-gather.15.cloned.1.call-start = ((), (), s32[]{:S(2)}) async-start(), calls=%async_computation.13 | async-start | bytes 2359296 | tf_op jit(solution)/shard_map/all_gather | solution.py:76
  301.7 128.3 %all-gather.13.cloned.1.call-start = ((), (), s32[]{:S(2)}) async-start(), calls=%async_computation.12 | async-start | bytes 5242880 | tf_op jit(solution)/shard_map/all_gather | solution.py:58
  348.5 133.0 %all-gather.17.cloned.1.call-start = ((), (), s32[]{:S(2)}) async-start(), calls=%async_computation.14 | async-start | bytes 2359296 | tf_op jit(solution)/shard_map/all_gather | solution.py:77
  349.1 167.0 %all-gather.19.cloned.1.call-start = ((), (), s32[]{:S(2)}) async-start(), calls=%async_computation.16 | async-start | bytes 5242880 | tf_op jit(solution)/shard_map/all_gather | solution.py:58
  349.9 233.6 %reduce-scatter.17.cloned.1.call-start = ((), (), s32[]{:S(2)}) async-start(), calls=%async_computation.17 | async-start | bytes 5242880 | tf_op jit(solution)/shard_map/reduce_scatter | solution.py:62
  390.4 148.7 %copy-start.33 = (f32[1,1024]{1,0:T(1,128)}, f32[1,1024]{1,0:T(1,128)S(1)}, u32[]{:S(2)}) copy-start(f32[1,1024]{1,0:T(1,128)S(1)} %constant_dynamic-slice_fusion.2) | copy-start | bytes 12292
  538.8 91.7 %reduce-scatter.15.cloned.1.call-start = ((), (), s32[]{:S(2)}) async-start(), calls=%async_computation.15 | async-start | bytes 5242880 | tf_op jit(solution)/shard_map/reduce_scatter | solution.py:62
  550.8 79.7 %copy-start.25 = (f32[1,1024]{1,0:T(1,128)S(1)}, f32[1,1024]{1,0:T(1,128)}, u32[]{:S(2)}) copy-start(f32[1,1024]{1,0:T(1,128)} %get-tuple-element.295) | copy-start | bytes 12292
  550.9 121.3 %all-gather.21.cloned.1.call-start = ((), (), s32[]{:S(2)}) async-start(), calls=%async_computation.18 | async-start | bytes 5242880 | tf_op jit(solution)/shard_map/all_gather | solution.py:58
  635.1 37.1 %copy-start.14 = (bf16[1024,256]{1,0:T(8,128)(2,1)S(1)}, bf16[1024,256]{1,0:T(8,128)(2,1)}, u32[]{:S(2)}) copy-start(bf16[1024,256]{1,0:T(8,128)(2,1)} %all_gather.39) | copy-start | bytes 1572868
  637.6 435.0 %reduce-scatter.19.cloned.1.call-start = ((), (), s32[]{:S(2)}) async-start(), calls=%async_computation.19 | async-start | bytes 5242880 | tf_op jit(solution)/shard_map/reduce_scatter | solution.py:62
  1027.9 186.9 %reduce-scatter.27.cloned.1.call-start = ((), (), s32[]{:S(2)}) async-start(), calls=%async_computation.23 | async-start | bytes 2162688
  1030.6 273.2 %reduce-scatter.23.cloned.1.call-start = ((), (), s32[]{:S(2)}) async-start(), calls=%async_computation.21 | async-start | bytes 4718592 | tf_op jit(solution)/shard_map/reduce_scatter | solution.py:273
  1044.0 31.4 %copy-start.27 = (f32[1024]{0:T(1024)S(1)}, f32[1024]{0:T(1024)}, u32[]{:S(2)}) copy-start(f32[1024]{0:T(1024)} %get-tuple-element.227) | copy-start | bytes 12292
  1044.0 31.4 %copy-start.28 = (f32[1024]{0:T(1024)S(1)}, f32[1024]{0:T(1024)}, u32[]{:S(2)}) copy-start(f32[1024]{0:T(1024)} %get-tuple-element.233) | copy-start | bytes 12292
  1044.0 31.4 %copy-start.29 = (f32[1024]{0:T(1024)S(1)}, f32[1024]{0:T(1024)}, u32[]{:S(2)}) copy-start(f32[1024]{0:T(1024)} %get-tuple-element.285) | copy-start | bytes 12292
  1044.0 31.4 %copy-start.30 = (f32[1024]{0:T(1024)S(1)}, f32[1024]{0:T(1024)}, u32[]{:S(2)}) copy-start(f32[1024]{0:T(1024)} %get-tuple-element.294) | copy-start | bytes 12292
  1044.0 395.5 %reduce-scatter.25.cloned.1.call-start = ((), (), s32[]{:S(2)}) async-start(), calls=%async_computation.22 | async-start | bytes 540672
  1076.5 451.3 %reduce-scatter.21.cloned.1.call-start = ((), (), s32[]{:S(2)}) async-start(), calls=%async_computation.20 | async-start | bytes 4718592 | tf_op jit(solution)/shard_map/reduce_scatter | solution.py:272
  1103.4 208.3 %copy-start.10 = (f32[512,1024]{1,0:T(8,128)S(1)}, f32[512,1024]{1,0:T(8,128)}, u32[]{:S(2)}) copy-start(f32[512,1024]{1,0:T(8,128)} %copy-done.9) | copy-start | bytes 6291460
  1103.4 202.4 %all-to-all-start = ((bf16[8,128,1024]{1,2,0:T(8,128)(2,1)}), bf16[8,128,1024]{1,2,0:T(8,128)(2,1)}, u32[]{:S(2)}, u32[]{:S(2)}) async-start(bf16[8,128,1024]{1,2,0:T(8,128)(2,1)} %copy.73), calls=%async_computation.4 | async-start | bytes 4194304 | tf_op jit(solution)/shard_map/all_to_all | solution.py:20
  (38 other events, 312.8 us)
Sparse Core Ops, SparseCore 0:
  10.7 48.1 all-gather.10
  61.0 33.1 all-gather.8
  301.2 42.1 reduce-scatter.12
  345.6 49.2 all-gather.14
  397.0 32.9 all-gather.12
  432.2 49.2 all-gather.16
  483.1 32.9 all-gather.18
  539.0 44.4 reduce-scatter.16
  586.0 44.4 reduce-scatter.14
  637.7 34.4 all-gather.20
  1028.0 44.5 reduce-scatter.18
  1074.7 140.0 reduce-scatter.26
  1218.8 84.8 reduce-scatter.22
  1305.9 133.5 reduce-scatter.24
  1444.0 83.7 reduce-scatter.20
where the time goes:
time: 1540 us; the launch traced here: 1530 us
  waiting for transfers between devices  702 us (46%)
  local copies, waits for them, and re-layouts  291 us (19%)
  matrix products  275 us (18%)
  blocking collectives  119 us (8%)
  other arithmetic  106 us (7%)
  loops' own time  18.6 us (1%)
    unnamed x17, waiting for transfers between devices  232 us
    broadcast_in_dim x16, local copies, waits for them, and re-layouts, tile_scores(): scores = jnp.where(keep_mask, scores, NEGATIVE)  226 us
    reduce_scatter x4, waiting for transfers between devices, sum_rows(): lax.psum_scatter(partial_rows.astype(jnp.bfloat16), 'tensor', scatter_dim...  146 us
    all_gather x4, waiting for transfers between devices, gather_rows(): return lax.all_gather(local_rows, 'tensor', axis=0, tiled=True)  104 us
    reduce_scatter x1, waiting for transfers between devices, per_device(): lax.psum_scatter(grad_down, 'dp', scatter_dimension=0, tiled=True)  87.6 us
    reduce_scatter x1, waiting for transfers between devices, per_device(): lax.psum_scatter(grad_up, 'dp', scatter_dimension=0, tiled=True)  86.9 us
    dot_general x8, matrix products, tile_scores(): jnp.einsum('qhd,khd->hqk', query_tile, key_rows, preferred_element_type=j...  73.4 us
    convert_element_type x4, other arithmetic, one_tile(): (probabilities * (grad_probs - row_inner)).astype(jnp.bfloat16)  45.9 us
  transfers between devices with their start and end apart: 16, of which 13 were waited for; matrix products, arithmetic and copies ran while one was open for 6% of the time, Pallas kernels for 0%

commit v1 on v0

--- a/solution.py
+++ b/solution.py
@@ -8,6 +8,27 @@
 BLOCK = 64
 EPS = 1e-05
 NEGATIVE = -1e30
+
+
+def collect(shard, axis, dim):
+    size, index, width = (lax.axis_size(axis), lax.axis_index(axis), shard.shape[dim])
+    ahead = [(i, (i + 1) % size) for i in range(size)]
+    left = [(i, (i - 1) % size) for i in range(size)]
+    out = jnp.zeros((*shard.shape[:dim], size * width, *shard.shape[dim + 1 :]), shard.dtype)
+    out = lax.dynamic_update_slice_in_dim(out, shard, index * width, axis=dim)
+    from_left = from_right = shard
+    half = size // 2
+    for lap in range(1, half + 1):
+        from_left = lax.ppermute(from_left, axis, ahead)
+        out = lax.dynamic_update_slice_in_dim(
+            out, from_left, (index - lap) % size * width, axis=dim
+        )
+        if lap < size - half:
+            from_right = lax.ppermute(from_right, axis, left)
+            out = lax.dynamic_update_slice_in_dim(
+                out, from_right, (index + lap) % size * width, axis=dim
+            )
+    return out
 
 
 def in_blocks(value, dim, count):
@@ -65,10 +86,7 @@
 
 
 def attention_weights(qkv_weight, out_weight):
-    return (
-        lax.all_gather(qkv_weight, "dp", axis=0, tiled=True),
-        lax.all_gather(out_weight, "dp", axis=0, tiled=True),
-    )
+    return (lax.all_gather(qkv_weight, "dp", axis=0, tiled=True), collect(out_weight, "dp", 0))
 
 
 def feed_weights(up_weight, down_weight):

time: 1540 us -> 1540 us (level)
  blocking collectives: 119 us -> 84.7 us
  waiting for transfers between devices: 702 us -> 721 us
    all_gather x1 -> x0, blocking collectives: 33.9 us -> none  [attention_weights(): lax.all_gather(out_weight, 'dp', axis=0, tiled=True)]
  transfers between devices with their start and end apart: 16 -> 23, of which waited for: 13 -> 18; matrix products, arithmetic and copies ran while one was open for 6% -> 7% of each run, Pallas kernels for 0% -> 0%
where the time goes in v1:
time: 1540 us
  waiting for transfers between devices  721 us (47%)
  local copies, waits for them, and re-layouts  297 us (19%)
  matrix products  275 us (18%)
  other arithmetic  106 us (7%)
  blocking collectives  84.7 us (6%)
  loops' own time  19.1 us (1%)
  starting transfers between devices  17.2 us (1%)
    unnamed x17, waiting for transfers between devices  233 us
    broadcast_in_dim x16, local copies, waits for them, and re-layouts, tile_scores(): scores = jnp.where(keep_mask, scores, NEGATIVE)  225 us
    reduce_scatter x4, waiting for transfers between devices, sum_rows(): lax.psum_scatter(partial_rows.astype(jnp.bfloat16), 'tensor', scatter_dim...  148 us
    all_gather x4, waiting for transfers between devices, gather_rows(): return lax.all_gather(local_rows, 'tensor', axis=0, tiled=True)  108 us
    reduce_scatter x1, waiting for transfers between devices, per_device(): lax.psum_scatter(grad_down, 'dp', scatter_dimension=0, tiled=True)  87.2 us
    reduce_scatter x1, waiting for transfers between devices, per_device(): lax.psum_scatter(grad_up, 'dp', scatter_dimension=0, tiled=True)  87.1 us
    dot_general x8, matrix products, tile_scores(): jnp.einsum('qhd,khd->hqk', query_tile, key_rows, preferred_element_type=j...  72.9 us
    convert_element_type x4, other arithmetic, one_tile(): (probabilities * (grad_probs - row_inner)).astype(jnp.bfloat16)  45.9 us
  transfers between devices with their start and end apart: 23, of which 18 were waited for; matrix products, arithmetic and copies ran while one was open for 7% of the time, Pallas kernels for 0%

profile of v1, /device:TPU:0, one launch (start us, length us, event | category | flops | bytes accessed | tf_op | source)
XLA Modules:
  0.0 1536.0 jit_solution(14438605661853323666)
XLA Ops:
  9.1 44.2 %all-gather = f32[32,32,8]{1,2,0:T(8,128)S(1)} all-gather(f32[1,32,8]{1,2,0:T(8,128)} %bitcast.196), channel_id=1, replica_groups=mesh['dp'=8,'tensor'=4] {'dp','tensor'}, dimensions={0}, use_global_device_ids=true | all-gather | bytes 33792 | tf_op jit(solution)/shard_map/all_gather | solution.py:233
  102.8 192.3 %while.28 = (s32[]{:T(128)}, bf16[4,512,256]{2,1,0:T(8,128)(2,1)}, f32[4,4,512]{2,1,0:T(4,128)S(1)}, s32[4]{0:T(128)S(1)}, pred[4,32,32]{2,1,0:T(8,128)(4,1)S(1)...) while((s32[]{:T(128)}, bf16[4,512,256]{2,1,0:T(8,128)(2,1)}, ...), condition=%wide.region_6.7_spmd.clone, body=%wide.region_3.6_spmd.clone.sunk | while | flops 1124272128 | bytes 96148904 | solution.py:159
  111.0 22.8 %broadcast_in_dim.121 = pred[4,512,2048]{2,1,0:T(32,128)(4,1)} reshape(pred[4,8,64,32,64]{4,3,2,1,0:T(32,128)(4,1)} %broadcast_in_dim.120) | data formatting | bytes 8388608 | tf_op jit(solution)/shard_map/while/body/eval_jaxpr/jit(_where)/broadcast_in_dim | solution.py:127
  159.1 22.8 %broadcast_in_dim.121 = pred[4,512,2048]{2,1,0:T(32,128)(4,1)} reshape(pred[4,8,64,32,64]{4,3,2,1,0:T(32,128)(4,1)} %broadcast_in_dim.120) | data formatting | bytes 8388608 | tf_op jit(solution)/shard_map/while/body/eval_jaxpr/jit(_where)/broadcast_in_dim | solution.py:127
  207.1 22.8 %broadcast_in_dim.121 = pred[4,512,2048]{2,1,0:T(32,128)(4,1)} reshape(pred[4,8,64,32,64]{4,3,2,1,0:T(32,128)(4,1)} %broadcast_in_dim.120) | data formatting | bytes 8388608 | tf_op jit(solution)/shard_map/while/body/eval_jaxpr/jit(_where)/broadcast_in_dim | solution.py:127
  255.2 22.8 %broadcast_in_dim.121 = pred[4,512,2048]{2,1,0:T(32,128)(4,1)} reshape(pred[4,8,64,32,64]{4,3,2,1,0:T(32,128)(4,1)} %broadcast_in_dim.120) | data formatting | bytes 8388608 | tf_op jit(solution)/shard_map/while/body/eval_jaxpr/jit(_where)/broadcast_in_dim | solution.py:127
  300.5 43.9 %reduce-scatter.13.cloned.1.call-done = bf16[512,1024]{1,0:T(8,128)(2,1)} async-done(((bf16[2048,1024]{1,0:T(8,128)(2,1)}), bf16[512,1024]{1,0:T(8,128)(2,1)}) %reduce-scatter.13.cloned.1.call-update) | async-done | bytes 1048592 | tf_op jit(solution)/shard_map/reduce_scatter | solution.py:83
  351.0 40.5 %all_gather.37 = f32[1,4096]{1,0:T(1,128)S(1)} all-gather(f32[1,128]{1,0:T(1,128)S(1)} %copy-done.34), channel_id=1, replica_groups=mesh['dp'=8,'tensor'=4] {'dp','tensor'}, dimensions={1}, use_global_device_ids=true | all-gather | bytes 16896 | tf_op jit(solution)/shard_map/all_gather | solution.py:234
  395.9 35.1 %all-gather.13.cloned.1.call-done = bf16[2048,1024]{1,0:T(8,128)(2,1)} async-done(((bf16[512,1024]{1,0:T(8,128)(2,1)}), bf16[2048,1024]{1,0:T(8,128)(2,1)}) %all-gather.13.cloned.1.call-update) | async-done | bytes 4194320 | tf_op jit(solution)/shard_map/all_gather | solution.py:79
  441.6 40.9 %all-gather.17.cloned.1.call-done = bf16[1024,1024]{1,0:T(8,128)(2,1)} async-done(((bf16[128,1024]{1,0:T(8,128)(2,1)}), bf16[1024,1024]{1,0:T(8,128)(2,1)}) %all-gather.17.cloned.1.call-update) | async-done | bytes 2097168 | tf_op jit(solution)/shard_map/all_gather | solution.py:95
  482.5 34.6 %all-gather.19.cloned.1.call-done = bf16[2048,1024]{1,0:T(8,128)(2,1)} async-done(((bf16[512,1024]{1,0:T(8,128)(2,1)}), bf16[2048,1024]{1,0:T(8,128)(2,1)}) %all-gather.19.cloned.1.call-update) | async-done | bytes 4194320 | tf_op jit(solution)/shard_map/all_gather | solution.py:79
  517.2 14.3 convert_reduce_fusion
  540.1 11.8 convolution_convert_fusion.2
  552.0 32.6 %reduce-scatter.17.cloned.1.call-done = bf16[512,1024]{1,0:T(8,128)(2,1)} async-done(((bf16[2048,1024]{1,0:T(8,128)(2,1)}), bf16[512,1024]{1,0:T(8,128)(2,1)}) %reduce-scatter.17.cloned.1.call-update) | async-done | bytes 1048592 | tf_op jit(solution)/shard_map/reduce_scatter | solution.py:83
  587.9 43.7 %reduce-scatter.15.cloned.1.call-done = bf16[512,1024]{1,0:T(8,128)(2,1)} async-done(((bf16[2048,1024]{1,0:T(8,128)(2,1)}), bf16[512,1024]{1,0:T(8,128)(2,1)}) %reduce-scatter.15.cloned.1.call-update) | async-done | bytes 1048592 | tf_op jit(solution)/shard_map/reduce_scatter | solution.py:83
  638.7 34.6 %all-gather.21.cloned.1.call-done = bf16[2048,1024]{1,0:T(8,128)(2,1)} async-done(((bf16[512,1024]{1,0:T(8,128)(2,1)}), bf16[2048,1024]{1,0:T(8,128)(2,1)}) %all-gather.21.cloned.1.call-update) | async-done | bytes 4194320 | tf_op jit(solution)/shard_map/all_gather | solution.py:79
  677.9 328.6 %while.29 = (s32[]{:T(128)}, f32[2048,4,64]{0,2,1:T(8,128)}, f32[2048,4,64]{0,2,1:T(8,128)}, bf16[4,512,4,64]{1,3,2,0:T(8,128)(2,1)}, s32[4]{0:T(128)S(1)}, /*in...) while((s32[]{:T(128)}, f32[2048,4,64]{0,2,1:T(8,128)}, ...), condition=%wide.region_16.17_spmd.clone, body=%wide.region_14.16_spmd.clone.sunk | while | flops 2725054464 | bytes 256294480 | solution.py:208
  688.4 22.8 %broadcast_in_dim.123 = pred[4,512,2048]{2,1,0:T(32,128)(4,1)} reshape(pred[4,8,64,32,64]{4,3,2,1,0:T(32,128)(4,1)} %broadcast_in_dim.122) | data formatting | bytes 8388608 | tf_op jit(solution)/shard_map/while/body/eval_jaxpr/jit(_where)/broadcast_in_dim | solution.py:127
  720.4 12.6 multiply_reduce_fusion.3
  733.0 11.5 multiply_convert_fusion.5
  769.9 22.8 %broadcast_in_dim.123 = pred[4,512,2048]{2,1,0:T(32,128)(4,1)} reshape(pred[4,8,64,32,64]{4,3,2,1,0:T(32,128)(4,1)} %broadcast_in_dim.122) | data formatting | bytes 8388608 | tf_op jit(solution)/shard_map/while/body/eval_jaxpr/jit(_where)/broadcast_in_dim | solution.py:127
  801.9 12.6 multiply_reduce_fusion.3
  852.1 22.8 %broadcast_in_dim.123 = pred[4,512,2048]{2,1,0:T(32,128)(4,1)} reshape(pred[4,8,64,32,64]{4,3,2,1,0:T(32,128)(4,1)} %broadcast_in_dim.122) | data formatting | bytes 8388608 | tf_op jit(solution)/shard_map/while/body/eval_jaxpr/jit(_where)/broadcast_in_dim | solution.py:127
  884.1 12.6 multiply_reduce_fusion.3
  934.3 22.8 %broadcast_in_dim.123 = pred[4,512,2048]{2,1,0:T(32,128)(4,1)} reshape(pred[4,8,64,32,64]{4,3,2,1,0:T(32,128)(4,1)} %broadcast_in_dim.122) | data formatting | bytes 8388608 | tf_op jit(solution)/shard_map/while/body/eval_jaxpr/jit(_where)/broadcast_in_dim | solution.py:127
  966.3 12.6 multiply_reduce_fusion.3
  1031.8 13.3 convolution_bitcast_fusion
  1045.9 27.8 %reduce-scatter.19.cloned.1.call-done = bf16[512,1024]{1,0:T(8,128)(2,1)} async-done(((bf16[2048,1024]{1,0:T(8,128)(2,1)}), bf16[512,1024]{1,0:T(8,128)(2,1)}) %reduce-scatter.19.cloned.1.call-update) | async-done | bytes 1048592 | tf_op jit(solution)/shard_map/reduce_scatter | solution.py:83
  1110.2 106.1 %reduce-scatter.27.cloned.1.call-done = f32[128,1]{1,0:T(8,128)} async-done(((f32[4096,1]{1,0:T(8,128)}), f32[128,1]{1,0:T(8,128)}) %reduce-scatter.27.cloned.1.call-update) | async-done | bytes 528
  1217.8 87.2 %reduce-scatter.23.cloned.1.call-done = f32[128,1024]{0,1:T(8,128)} async-done(((f32[1024,1024]{0,1:T(8,128)}), f32[128,1024]{0,1:T(8,128)}) %reduce-scatter.23.cloned.1.call-update) | async-done | bytes 524304 | tf_op jit(solution)/shard_map/reduce_scatter | solution.py:291
  1315.9 124.9 %reduce-scatter.25.cloned.1.call-done = f32[32,8]{1,0:T(8,128)} async-done(((f32[1024,8]{1,0:T(8,128)}), f32[32,8]{1,0:T(8,128)}) %reduce-scatter.25.cloned.1.call-update) | async-done | bytes 1040
  1442.2 87.1 %reduce-scatter.21.cloned.1.call-done = f32[128,1024]{1,0:T(8,128)} async-done(((f32[1024,1024]{1,0:T(8,128)}), f32[128,1024]{1,0:T(8,128)}) %reduce-scatter.21.cloned.1.call-update) | async-done | bytes 524304 | tf_op jit(solution)/shard_map/reduce_scatter | solution.py:290
  (337 shorter events, 434.7 us)
Async XLA Ops:
  7.2 53.3 %copy-start.16 = (bf16[128,256]{1,0:T(8,128)(2,1)S(1)}, bf16[128,256]{1,0:T(8,128)(2,1)}, u32[]{:S(2)}) copy-start(bf16[128,256]{1,0:T(8,128)(2,1)} %param.21) | copy-start | bytes 196612
  7.2 56.1 %copy-start.30 = (s32[1,4,32,3]{2,1,3,0:T(4,128)S(1)}, s32[1,4,32,3]{2,1,3,0:T(4,128)}, u32[]{:S(2)}) copy-start(s32[1,4,32,3]{2,1,3,0:T(4,128)} %param.19) | copy-start | bytes 4612
  7.2 56.2 %copy-start.29 = (s32[1,32]{1,0:T(1,128)S(1)}, s32[1,32]{1,0:T(1,128)}, u32[]{:S(2)}) copy-start(s32[1,32]{1,0:T(1,128)} %param.18) | copy-start | bytes 388
  7.2 83.8 %all-gather.11.cloned.1.call-start = ((), (), s32[]{:S(2)}) async-start(), calls=%async_computation.10 | async-start | bytes 1769472 | tf_op jit(solution)/shard_map/all_gather | solution.py:89
  9.0 86.0 %all-gather.9.cloned.1.call-start = ((), (), s32[]{:S(2)}) async-start(), calls=%async_computation.9 | async-start | bytes 5242880 | tf_op jit(solution)/shard_map/all_gather | solution.py:79
  60.4 283.9 %reduce-scatter.13.cloned.1.call-start = ((), (), s32[]{:S(2)}) async-start(), calls=%async_computation.11 | async-start | bytes 5242880 | tf_op jit(solution)/shard_map/reduce_scatter | solution.py:83
  60.5 5.7 collective-permute-start.1
  60.6 8.4 collective-permute-start
  66.2 4.7 collective-permute-start.3
  69.0 7.1 collective-permute-start.2
  70.9 13.2 collective-permute-start.5
  76.0 7.0 collective-permute-start.4
  83.0 7.4 collective-permute-start.6
  299.7 44.7 %copy-start.14 = (f32[1,1024]{1,0:T(1,128)S(1)}, f32[1,1024]{1,0:T(1,128)}, u32[]{:S(2)}) copy-start(f32[1,1024]{1,0:T(1,128)} %get-tuple-element.298) | copy-start | bytes 12292
  299.7 48.3 %copy-start.15 = (f32[1,1024]{1,0:T(1,128)S(1)}, f32[1,1024]{1,0:T(1,128)}, u32[]{:S(2)}) copy-start(f32[1,1024]{1,0:T(1,128)} %get-tuple-element.297) | copy-start | bytes 12292
  299.7 48.3 %copy-start.24 = (f32[1,1024]{1,0:T(1,128)S(1)}, f32[1,1024]{1,0:T(1,128)}, u32[]{:S(2)}) copy-start(f32[1,1024]{1,0:T(1,128)} %get-tuple-element.296) | copy-start | bytes 12292
  299.7 96.2 %all-gather.15.cloned.1.call-start = ((), (), s32[]{:S(2)}) async-start(), calls=%async_computation.13 | async-start | bytes 2359296 | tf_op jit(solution)/shard_map/all_gather | solution.py:94
  300.3 130.7 %all-gather.13.cloned.1.call-start = ((), (), s32[]{:S(2)}) async-start(), calls=%async_computation.12 | async-start | bytes 5242880 | tf_op jit(solution)/shard_map/all_gather | solution.py:79
  349.6 133.0 %all-gather.17.cloned.1.call-start = ((), (), s32[]{:S(2)}) async-start(), calls=%async_computation.14 | async-start | bytes 2359296 | tf_op jit(solution)/shard_map/all_gather | solution.py:95
  350.1 167.0 %all-gather.19.cloned.1.call-start = ((), (), s32[]{:S(2)}) async-start(), calls=%async_computation.16 | async-start | bytes 5242880 | tf_op jit(solution)/shard_map/all_gather | solution.py:79
  350.9 233.7 %reduce-scatter.17.cloned.1.call-start = ((), (), s32[]{:S(2)}) async-start(), calls=%async_computation.17 | async-start | bytes 5242880 | tf_op jit(solution)/shard_map/reduce_scatter | solution.py:83
  391.4 148.7 %copy-start.31 = (f32[1,1024]{1,0:T(1,128)}, f32[1,1024]{1,0:T(1,128)S(1)}, u32[]{:S(2)}) copy-start(f32[1,1024]{1,0:T(1,128)S(1)} %constant_dynamic-slice_fusion.2) | copy-start | bytes 12292
  539.9 91.7 %reduce-scatter.15.cloned.1.call-start = ((), (), s32[]{:S(2)}) async-start(), calls=%async_computation.15 | async-start | bytes 5242880 | tf_op jit(solution)/shard_map/reduce_scatter | solution.py:83
  551.9 79.7 %copy-start.23 = (f32[1,1024]{1,0:T(1,128)S(1)}, f32[1,1024]{1,0:T(1,128)}, u32[]{:S(2)}) copy-start(f32[1,1024]{1,0:T(1,128)} %get-tuple-element.295) | copy-start | bytes 12292
  551.9 121.4 %all-gather.21.cloned.1.call-start = ((), (), s32[]{:S(2)}) async-start(), calls=%async_computation.18 | async-start | bytes 5242880 | tf_op jit(solution)/shard_map/all_gather | solution.py:79
  638.6 435.1 %reduce-scatter.19.cloned.1.call-start = ((), (), s32[]{:S(2)}) async-start(), calls=%async_computation.19 | async-start | bytes 5242880 | tf_op jit(solution)/shard_map/reduce_scatter | solution.py:83
  1029.0 187.3 %reduce-scatter.27.cloned.1.call-start = ((), (), s32[]{:S(2)}) async-start(), calls=%async_computation.23 | async-start | bytes 2162688
  1031.7 273.3 %reduce-scatter.23.cloned.1.call-start = ((), (), s32[]{:S(2)}) async-start(), calls=%async_computation.21 | async-start | bytes 4718592 | tf_op jit(solution)/shard_map/reduce_scatter | solution.py:291
  1045.2 395.6 %reduce-scatter.25.cloned.1.call-start = ((), (), s32[]{:S(2)}) async-start(), calls=%async_computation.22 | async-start | bytes 540672
  1077.6 451.7 %reduce-scatter.21.cloned.1.call-start = ((), (), s32[]{:S(2)}) async-start(), calls=%async_computation.20 | async-start | bytes 4718592 | tf_op jit(solution)/shard_map/reduce_scatter | solution.py:290
  1104.6 208.4 %copy-start.10 = (f32[512,1024]{1,0:T(8,128)S(1)}, f32[512,1024]{1,0:T(8,128)}, u32[]{:S(2)}) copy-start(f32[512,1024]{1,0:T(8,128)} %copy-done.9) | copy-start | bytes 6291460
  1104.6 202.5 %all-to-all-start = ((bf16[8,128,1024]{1,2,0:T(8,128)(2,1)}), bf16[8,128,1024]{1,2,0:T(8,128)(2,1)}, u32[]{:S(2)}, u32[]{:S(2)}) async-start(bf16[8,128,1024]{1,2,0:T(8,128)(2,1)} %copy.73), calls=%async_computation.4 | async-start | bytes 4194304 | tf_op jit(solution)/shard_map/all_to_all | solution.py:41
  (43 other events, 483.2 us)
Sparse Core Ops, SparseCore 0:
  10.7 49.4 all-gather.10
  62.3 32.6 all-gather.8
  299.8 44.5 reduce-scatter.12
  346.6 49.2 all-gather.14
  398.0 32.9 all-gather.12
  433.2 49.2 all-gather.16
  484.2 32.9 all-gather.18
  540.0 44.5 reduce-scatter.16
  587.1 44.4 reduce-scatter.14
  638.8 34.4 all-gather.20
  1029.2 44.5 reduce-scatter.18
  1075.8 140.5 reduce-scatter.26
  1220.4 84.5 reduce-scatter.22
  1307.1 133.6 reduce-scatter.24
  1445.3 83.9 reduce-scatter.20
